TPU v7x, 256 devices: a whole 4x4x8 slice. The times are simulated.
256 devices in a mesh: row: 32 (over x, y, core), col: 8 (over z).
Axes of the slice: x: 4, y: 4, z: 8, core: 2. Of those that a mesh axis runs over, the one named last changes fastest.
Arguments:
- a_matrix: float32 [2048, 2048], P('row', 'col'), may hold values from -0.9 to 0.9
- b_matrix: float32 [2048, 2048], P('row', 'col'), may hold values from -0.9 to 0.9
- a_panel: float32 [2048, 1024], P('row', 'col'), may hold values from -0.9 to 0.9
- b_panel: float32 [2048, 1024], P('row', 'col'), may hold values from -0.9 to 0.9
Outputs:
- triangle: float32 [1024, 1024], P('row', 'col')
- pencil_cross: float32 [2048, 2048], P('row', 'col')
All inputs are finite; a program needn't handle non-finite values.
Results may differ from a plain program's by a relative error of at most 0.0003.
Values sent between devices are 32-bit elements; how exact they have to be, the bound alone decides.
A program may use at most 64 MiB of HBM per device.

v0:
```python
import jax
import jax.numpy as jnp
from jax import lax
from jax.sharding import PartitionSpec as P

HIGHEST = lax.Precision.HIGHEST


def in_one_piece(arrays, axis, dim, along):
    widths = [a.shape[along] for a in arrays]
    both = jnp.concatenate(arrays, axis=along)
    whole = lax.all_gather(both, axis, axis=dim, tiled=True)
    return tuple(jnp.split(whole, [sum(widths[:k]) for k in range(1, len(widths))], axis=along))


def in_blocks(x, dim, count):
    lengths = x.shape
    blocks = x.reshape(*lengths[:dim], count, lengths[dim] // count, *lengths[dim + 1 :])
    return jnp.moveaxis(blocks, dim, 0)


def summed_on_arrival(x, axis, dim):
    blocks = in_blocks(x, dim, lax.axis_size(axis))
    arrived = lax.all_to_all(blocks, axis, split_axis=0, concat_axis=0, tiled=True)
    return arrived.sum(axis=0)


def from_everyone(x, axis):
    count = lax.axis_size(axis)
    return lax.all_to_all(jnp.broadcast_to(x[None], (count, *x.shape)), axis, 0, 0, tiled=True)


def joined_along(blocks, dim):
    blocks = jnp.moveaxis(blocks, 0, dim)
    lengths = blocks.shape
    return blocks.reshape(*lengths[:dim], lengths[dim] * lengths[dim + 1], *lengths[dim + 2 :])


def gather_directly(x, axis, dim):
    blocks = from_everyone(x, axis)
    return joined_along(blocks, dim)


def local(a_matrix, b_matrix, a_panel, b_panel):
    row_count = a_matrix.shape[0]
    panel_width = a_panel.shape[1]
    full_a, full_pa, full_pb = (
        lax.all_gather(a_matrix, "col", axis=1, tiled=True),
        *in_one_piece((a_panel, b_panel), "col", 1, 0),
    )
    stacked = jnp.concatenate([full_pb, -full_pa], 0)
    own_block = jnp.concatenate([b_panel, -a_panel], 0)
    partial_gram = jnp.dot(own_block.T, stacked, precision=HIGHEST)
    gram_part = summed_on_arrival(partial_gram, "row", 1)
    gram_rows = gather_directly(gram_part, "row", 1)
    gram_matrix = lax.all_gather(gram_rows, "col", axis=0, tiled=True)
    lower_factor = jnp.linalg.cholesky(gram_matrix)
    q_rows = jax.scipy.linalg.solve_triangular(lower_factor, stacked.T, lower=True).T
    upper_rows = q_rows[:row_count]
    lower_rows = q_rows[row_count:]
    row_index = lax.axis_index("row")
    col_index = lax.axis_index("col")
    tri_rows = gram_matrix.shape[0] // lax.axis_size("row")
    corner = lax.dynamic_slice(
        lower_factor, (col_index * panel_width, row_index * tri_rows), (panel_width, tri_rows)
    )
    triangle = corner.T
    partial_z = jnp.dot(lower_rows.T, b_matrix, precision=HIGHEST)
    z_part = summed_on_arrival(partial_z, "row", 0)
    z_columns = gather_directly(z_part, "row", 0)
    v_block = jnp.dot(upper_rows, z_columns, precision=HIGHEST)
    pencil_cross = summed_on_arrival(-jnp.dot(full_a.T, v_block, precision=HIGHEST), "row", 0)
    return (triangle, pencil_cross)


def solution(mesh):
    in_specs = (P("row", "col"), P("row", "col"), P("row", "col"), P("row", "col"))
    out_specs = (P("row", "col"), P("row", "col"))
    return jax.shard_map(local, mesh=mesh, in_specs=in_specs, out_specs=out_specs, check_vma=False)
```

profile of v0, /device:TPU:3, one launch (start us, length us, event | category | flops | bytes accessed | tf_op | source)
XLA Modules:
  0.0 571.6 jit_solution(9497342517812801916)
XLA Ops:
  8.8 22.9 %all_gather.9 = f32[128,1024]{1,0:T(8,128)S(1)} all-gather(f32[128,128]{1,0:T(8,128)S(1)} %pad_maximum_fusion.2), channel_id=1, replica_groups=mesh['row'=32,'col'=8] {'col'}, dimensions={1}, use_global_device_ids=true | all-gather | bytes 589824 | tf_op jit(solution)/shard_map/all_gather | solution.py:12
  33.5 24.3 %all_to_all.25 = f32[32,128,32]{1,2,0:T(8,128)S(1)} all-to-all(f32[32,128,32]{1,2,0:T(8,128)S(1)} %bitcast.125), channel_id=1, replica_groups=mesh['row'=32,'col'=8] {'row'}, dimensions={0} | all-to-all | bytes 1048576 | tf_op jit(solution)/shard_map/all_to_all | solution.py:24
  57.9 15.1 %all_to_all.26 = f32[32,128,32]{1,2,0:T(8,128)} all-to-all(f32[32,128,32]{1,2,0:T(8,128)S(1)} %broadcast_in_dim.6), channel_id=1, replica_groups=mesh['row'=32,'col'=8] {'row'}, dimensions={0} | all-to-all | bytes 1048576 | tf_op jit(solution)/shard_map/all_to_all | solution.py:30
  73.1 54.4 %all-gather.2.cloned.1.call-done = f32[1024,1024]{0,1:T(8,128)} async-done(((f32[128,1024]{0,1:T(8,128)}), f32[1024,1024]{0,1:T(8,128)}) %all-gather.2.cloned.1.call-update) | async-done | bytes 4194320 | tf_op jit(solution)/shard_map/all_gather | solution.py:56
  127.5 5.5 copy.16
  133.0 4.4 fusion
  139.4 11.7 %cholesky.223 = f32[128,128]{1,0:T(8,128)S(1)} custom-call(f32[128,128]{1,0:T(8,128)S(1)} %cholesky.580), custom_call_target="Cholesky" | custom-call | tf_op jit(solution)/shard_map/jit(cholesky)/cholesky | solution.py:57
  151.2 2.5 cholesky.255
  153.7 9.8 %custom-call.63 = f32[1,128,128]{1,2,0:T(8,128)S(1)} custom-call(f32[1,128,128]{2,1,0:T(8,128)S(1)} %get-tuple-element.74), custom_call_target="InvertDiagBlocksLowerTriangular" | custom-call | tf_op jit(solution)/shard_map/jit(cholesky)/cholesky | solution.py:57
  167.3 11.9 %cholesky.244 = f32[128,128]{1,0:T(8,128)S(1)} custom-call(f32[128,128]{1,0:T(8,128)S(1)} %cholesky.584), custom_call_target="Cholesky" | custom-call | tf_op jit(solution)/shard_map/jit(cholesky)/cholesky | solution.py:57
  180.7 9.8 %custom-call.64 = f32[1,128,128]{1,2,0:T(8,128)S(1)} custom-call(f32[1,128,128]{2,1,0:T(8,128)S(1)} %get-tuple-element.71), custom_call_target="InvertDiagBlocksLowerTriangular" | custom-call | tf_op jit(solution)/shard_map/jit(cholesky)/cholesky | solution.py:57
  193.8 11.7 %cholesky.468 = f32[128,128]{1,0:T(8,128)S(1)} custom-call(f32[128,128]{1,0:T(8,128)S(1)} %cholesky.589), custom_call_target="Cholesky" | custom-call | tf_op jit(solution)/shard_map/jit(cholesky)/cholesky | solution.py:57
  206.8 9.8 %custom-call.65 = f32[1,128,128]{1,2,0:T(8,128)S(1)} custom-call(f32[1,128,128]{2,1,0:T(8,128)S(1)} %get-tuple-element.68), custom_call_target="InvertDiagBlocksLowerTriangular" | custom-call | tf_op jit(solution)/shard_map/jit(cholesky)/cholesky | solution.py:57
  217.8 2.3 convolution_subtract_fusion.2
  220.2 12.1 %cholesky.487 = f32[128,128]{1,0:T(8,128)S(1)} custom-call(f32[128,128]{1,0:T(8,128)S(1)} %cholesky.594), custom_call_target="Cholesky" | custom-call | tf_op jit(solution)/shard_map/jit(cholesky)/cholesky | solution.py:57
  233.6 9.8 %custom-call.66 = f32[1,128,128]{1,2,0:T(8,128)S(1)} custom-call(f32[1,128,128]{2,1,0:T(8,128)S(1)} %get-tuple-element.65), custom_call_target="InvertDiagBlocksLowerTriangular" | custom-call | tf_op jit(solution)/shard_map/jit(cholesky)/cholesky | solution.py:57
  244.5 2.3 convolution_subtract_fusion.3
  246.9 11.7 %cholesky.506 = f32[128,128]{1,0:T(8,128)S(1)} custom-call(f32[128,128]{1,0:T(8,128)S(1)} %cholesky.599), custom_call_target="Cholesky" | custom-call | tf_op jit(solution)/shard_map/jit(cholesky)/cholesky | solution.py:57
  259.9 10.0 %custom-call.67 = f32[1,128,128]{1,2,0:T(8,128)S(1)} custom-call(f32[1,128,128]{2,1,0:T(8,128)S(1)} %get-tuple-element.62), custom_call_target="InvertDiagBlocksLowerTriangular" | custom-call | tf_op jit(solution)/shard_map/jit(cholesky)/cholesky | solution.py:57
  273.2 11.7 %cholesky.526 = f32[128,128]{1,0:T(8,128)S(1)} custom-call(f32[128,128]{1,0:T(8,128)S(1)} %cholesky.604), custom_call_target="Cholesky" | custom-call | tf_op jit(solution)/shard_map/jit(cholesky)/cholesky | solution.py:57
  286.2 9.8 %custom-call.68 = f32[1,128,128]{1,2,0:T(8,128)S(1)} custom-call(f32[1,128,128]{2,1,0:T(8,128)S(1)} %get-tuple-element.59), custom_call_target="InvertDiagBlocksLowerTriangular" | custom-call | tf_op jit(solution)/shard_map/jit(cholesky)/cholesky | solution.py:57
  299.0 11.9 %cholesky.546 = f32[128,128]{1,0:T(8,128)S(1)} custom-call(f32[128,128]{1,0:T(8,128)S(1)} %cholesky.609), custom_call_target="Cholesky" | custom-call | tf_op jit(solution)/shard_map/jit(cholesky)/cholesky | solution.py:57
  312.2 9.8 %custom-call.69 = f32[1,128,128]{1,2,0:T(8,128)S(1)} custom-call(f32[1,128,128]{2,1,0:T(8,128)S(1)} %get-tuple-element.56), custom_call_target="InvertDiagBlocksLowerTriangular" | custom-call | tf_op jit(solution)/shard_map/jit(cholesky)/cholesky | solution.py:57
  324.6 11.7 %cholesky.564 = f32[128,128]{1,0:T(8,128)S(1)} custom-call(f32[128,128]{1,0:T(8,128)S(1)} %convolution_subtract_fusion.11), custom_call_target="Cholesky" | custom-call | tf_op jit(solution)/shard_map/jit(cholesky)/cholesky | solution.py:57
  343.3 6.6 %fusion.1 = (f32[1024,1024]{1,0:T(8,128)}, f32[1024,1024]{1,0:T(8,128)}) fusion(f32[1024,1024]{1,0:T(8,128)} %get-tuple-element.54, pred[]{:T(512)S(6)} %cholesky.579), kind=kLoop, calls=%fused_computation.6 | loop fusion | flops 4194304 | bytes 12582913 | tf_op jit(solution)/shard_map/jit(_solve_triangular)/triangular_solve | solution.py:58
  350.0 23.2 %while.1 = (s32[]{:T(128)}, f32[1024,1024]{1,0:T(8,128)}, s32[8,2]{0,1:T(2,128)S(1)}, f32[8,128,128]{2,1,0:T(8,128)S(1)}, s32[]{:T(128)}) while((s32[]{:T(128)}, f32[1024,1024]{1,0:T(8,128)}, s32[8,2]{0,1:T(2,128)S(1)}, f32[8,128,128]{2,1,0:T(8,128)S(1)}, s32[]{:T(128)}) %tuple.64), condition=%wide.while_cond, body=%wide.while_body.sunk | while | flops 2 | bytes 131181 | solution.py:58
  373.2 78.8 %custom-call.70 = f32[8,128,128]{1,2,0:T(8,128)S(1)} custom-call(f32[8,128,128]{2,1,0:T(8,128)S(1)} %get-tuple-element.9), custom_call_target="InvertDiagBlocksLowerTriangular" | custom-call | tf_op jit(solution)/shard_map/jit(_solve_triangular)/triangular_solve | solution.py:58
  466.3 26.9 %all_to_all.27 = f32[32,32,256]{2,1,0:T(8,128)S(1)} all-to-all(f32[32,32,256]{2,1,0:T(8,128)S(1)} %bitcast.121), channel_id=1, replica_groups=mesh['row'=32,'col'=8] {'row'}, dimensions={0} | all-to-all | bytes 2097152 | tf_op jit(solution)/shard_map/all_to_all | solution.py:24
  494.3 5.6 all-to-all-start.3
  500.0 20.2 %all_gather.11 = f32[64,2048]{1,0:T(8,128)S(1)} all-gather(f32[64,256]{1,0:T(8,128)S(1)} %copy-done.2), channel_id=1, replica_groups=mesh['row'=32,'col'=8] {'col'}, dimensions={1}, use_global_device_ids=true | all-gather | bytes 589824 | tf_op jit(solution)/shard_map/all_gather | solution.py:48
  525.0 12.5 %all-to-all-start.4 = ((f32[32,64,256]{2,1,0:T(8,128)}), f32[32,64,256]{2,1,0:T(8,128)S(1)}, u32[]{:S(2)}, u32[]{:S(2)}) async-start(f32[32,64,256]{2,1,0:T(8,128)} %bitcast.119), calls=%async_computation.4 | async-start | bytes 4194304 | tf_op jit(solution)/shard_map/all_to_all | solution.py:24
  539.1 24.4 %all-to-all-done.4 = f32[32,64,256]{2,1,0:T(8,128)S(1)} async-done(((f32[32,64,256]{2,1,0:T(8,128)}), f32[32,64,256]{2,1,0:T(8,128)S(1)}, u32[]{:S(2)}, u32[]{:S(2)}) %all-to-all-start.4) | async-done | bytes 2097184 | tf_op jit(solution)/shard_map/all_to_all | solution.py:24
  (103 shorter events, 79.3 us)
Async XLA Ops:
  7.2 458.1 %copy-start = (f32[64,256]{1,0:T(8,128)S(1)}, f32[64,256]{1,0:T(8,128)}, u32[]{:S(2)}) copy-start(f32[64,256]{1,0:T(8,128)} %param.5) | copy-start | bytes 196612
  7.2 120.4 %all-gather.2.cloned.1.call-start = ((), (), s32[]{:S(2)}) async-start(), calls=%async_computation.5 | async-start | bytes 4718592 | tf_op jit(solution)/shard_map/all_gather | solution.py:56
  137.5 1.9 copy-start.1
  464.9 35.1 %copy-start.2 = (f32[64,256]{1,0:T(8,128)S(1)}, f32[64,256]{1,0:T(8,128)}, u32[]{:S(2)}) copy-start(f32[64,256]{1,0:T(8,128)} %param.4) | copy-start | bytes 196612
  494.3 25.9 %all-to-all-start.3 = ((f32[32,32,256]{2,1,0:T(8,128)}), f32[32,32,256]{2,1,0:T(8,128)S(1)}, u32[]{:S(2)}, u32[]{:S(2)}) async-start(f32[32,32,256]{2,1,0:T(8,128)} %broadcast_in_dim.7), calls=%async_computation.3 | async-start | bytes 2097152 | tf_op jit(solution)/shard_map/all_to_all | solution.py:30
  525.0 38.5 %all-to-all-start.4 = ((f32[32,64,256]{2,1,0:T(8,128)}), f32[32,64,256]{2,1,0:T(8,128)S(1)}, u32[]{:S(2)}, u32[]{:S(2)}) async-start(f32[32,64,256]{2,1,0:T(8,128)} %bitcast.119), calls=%async_computation.4 | async-start | bytes 4194304 | tf_op jit(solution)/shard_map/all_to_all | solution.py:24
Sparse Core Ops, SparseCore 0:
  73.2 54.3 all-gather.1
where the time goes:
time: 579 us; the launch traced here: 572 us
  other arithmetic  265 us (46%)
  blocking collectives  109 us (19%)
  waiting for transfers between devices  78.9 us (14%)
  matrix products  41.5 us (7%)
  local copies, waits for them, and re-layouts  38.7 us (7%)
  between operations  19.9 us (3%)
  starting transfers between devices  18.2 us (3%)
    another operation x30, other arithmetic, local(): lower_factor = jnp.linalg.cholesky(gram_matrix)  172 us
    another operation x3, other arithmetic, local(): jax.scipy.linalg.solve_triangular(lower_factor, stacked.T, lower=True)  85.5 us
    all_gather x1, waiting for transfers between devices, local(): gram_matrix = lax.all_gather(gram_rows, 'col', axis=0, tiled=True)  54.4 us
    all_to_all x2, blocking collectives, summed_on_arrival(): lax.all_to_all(blocks, axis, split_axis=0, concat_axis=0, tiled=True)  51.2 us
    all_to_all x1, waiting for transfers between devices, summed_on_arrival(): lax.all_to_all(blocks, axis, split_axis=0, concat_axis=0, tiled=True)  24.4 us
    another operation x24, local copies, waits for them, and re-layouts  23 us
    all_gather x1, blocking collectives, in_one_piece(): whole = lax.all_gather(both, axis, axis=dim, tiled=True)  22.9 us
    another operation x14, matrix products, local(): lower_factor = jnp.linalg.cholesky(gram_matrix)  22.7 us
  transfers between devices with their start and end apart: 3, of which 2 were waited for; matrix products, arithmetic and copies ran while one was open for 0% of the time, Pallas kernels for 0%

commit v1 on v0

v1 whole, which is shorter than its diff:
```python
import jax
import jax.numpy as jnp
from jax import lax
from jax.experimental import pallas as pl
from jax.experimental.pallas import tpu as pltpu
from jax.sharding import PartitionSpec as P

HIGHEST = lax.Precision.HIGHEST
MESH = pl.DeviceIdType.MESH
B = 128
ROWS = 32
COLS = 8
CHIPS = 16
K = COLS * B
CD_STEP = 3


def dot_t(a, b):
    return lax.dot_general(
        a, b, (((0,), (0,)), ((), ())), precision=HIGHEST, preferred_element_type=jnp.float32
    )


def dot(a, b):
    return jnp.dot(a, b, precision=HIGHEST, preferred_element_type=jnp.float32)


def lane(x, k):
    return jnp.broadcast_to(x[:, k : k + 1], x.shape)


def sub(x, k):
    return jnp.broadcast_to(x[k : k + 1, :], x.shape)


def factor_block(d_ref, r_ref, li_ref):
    srow = lax.broadcasted_iota(jnp.int32, (8, B), 0)
    lcol = lax.broadcasted_iota(jnp.int32, (8, B), 1)
    groups = B // 8
    left = [d_ref[8 * g : 8 * g + 8, :] for g in range(groups)]
    right = [jnp.where(lcol == srow + 8 * g, 1.0, 0.0).astype(jnp.float32) for g in range(groups)]
    for i in range(groups):
        p, q = left[i], right[i]
        cols = [lane(p, 8 * i + m) for m in range(8)]
        rp = jnp.zeros((8, B), jnp.float32)
        rq = rp
        for m in range(8):
            pivot = sub(cols[m], m)
            inv = 1.0 / pivot
            root = lax.rsqrt(pivot)
            f = jnp.where(srow == m, 1.0 - inv, cols[m] * inv)
            pm, qm = sub(p, m), sub(q, m)
            rp = jnp.where(srow == m, pm * root, rp)
            rq = jnp.where(srow == m, qm * root, rq)
            p = p - f * pm
            q = q - f * qm
            for n in range(m + 1, 8):
                cols[n] = cols[n] - f * sub(cols[n], m)
        r_ref[8 * i : 8 * i + 8, :] = jnp.where(lcol >= srow + 8 * i, rp, 0.0)
        li_ref[8 * i : 8 * i + 8, :] = rq
        yp = [sub(p, m) for m in range(8)]
        yq = [sub(q, m) for m in range(8)]
        for g in range(i + 1, groups):
            c = [lane(left[g], 8 * i + m) for m in range(8)]
            u, v = left[g], right[g]
            for m in range(8):
                u = u - c[m] * yp[m]
                v = v - c[m] * yq[m]
            left[g], right[g] = u, v


def kernel(
    am, bm, ap, bp, tri, out,
    zb, pg, rg, sg, gw, pd, pcx, rd, rc, sd, sc, rhs, rr, lis, dd, dr, oo,
    z_s, z_r, g_s, g_r, y_s, y_r, a_s, a_r, p_s, p_r, d_s, d_r, c_s, c_r, e_s, e_r, f_s, f_r,
):
    k = lax.axis_index("row")
    n = lax.axis_index("col")
    t = k // 2
    core = lax.rem(k, 2)

    barrier = pltpu.get_barrier_semaphore()
    for s in range(1, COLS):
        pl.semaphore_signal(barrier, inc=1, device_id=(k, lax.rem(n + s, COLS)), device_id_type=MESH)
    for s in range(1, ROWS):
        pl.semaphore_signal(barrier, inc=1, device_id=(lax.rem(k + s, ROWS), n), device_id_type=MESH)
    pl.semaphore_wait(barrier, COLS - 1 + ROWS - 1)

    def send(src, dst, ssem, rsem, row, col):
        pltpu.make_async_remote_copy(
            src_ref=src, dst_ref=dst, send_sem=ssem, recv_sem=rsem, device_id=(row, col), device_id_type=MESH
        ).start()

    def local(src, dst, sem):
        pltpu.make_async_copy(src, dst, sem).start()

    def take(ref, sem):
        pltpu.make_async_copy(ref, ref, sem).wait()

    for s in (1, 7, 2, 6, 3, 5, 4):
        to = lax.rem(n + s, COLS)
        send(bp, zb.at[n, 0:64], z_s, z_r.at[n], k, to)
        send(ap, zb.at[n, 64:128], z_s, z_r.at[n], k, to)
    local(bp, zb.at[n, 0:64], z_r.at[n])
    local(ap, zb.at[n, 64:128], z_r.at[n])

    def near(s):
        return lax.rem(n + s + COLS, COLS)

    for s in (0, 1, -1, 2, -2):
        take(zb.at[near(s)], z_r.at[near(s)])

    lows, highs, mine = [], [], []
    for d in range(5):
        i, j = near(-(d // 2)), near((d + 1) // 2)
        lo, hi = jnp.minimum(i, j), jnp.maximum(i, j)
        lows.append(lo)
        highs.append(hi)
        mine.append(lax.rem(lo, 2) == core)
    for d in range(5):
        def share(d=d):
            pg[d] = dot_t(zb[lows[d]], zb[highs[d]])
            to_core = lax.rem(lows[d], 2)
            for s in range(1, CHIPS):
                to = lax.rem(t + s, CHIPS)
                send(pg.at[d, pl.ds(pl.multiple_of(8 * to, 8), 8)], rg.at[d, k], g_s.at[d], g_r.at[d], 2 * to + to_core, n)
            own = pg.at[d, pl.ds(pl.multiple_of(8 * t, 8), 8)]

            @pl.when(mine[d])
            def _():
                local(own, rg.at[d, k], g_r.at[d])

            @pl.when(jnp.logical_not(mine[d]))
            def _():
                send(own, rg.at[d, k], g_s.at[d], g_r.at[d], 2 * t + 1 - core, n)

        if d < 4:
            share()
        else:
            pl.when(n < 4)(share)

    for s in (3, -3, 4):
        take(zb.at[near(s)], z_r.at[near(s)])
    for c in range(COLS):
        pd[c * B : (c + 1) * B, :] = dot_t(zb[c, 64:128, :], bm[...])
        pcx[c * B : (c + 1) * B, :] = dot_t(zb[c, 0:64, :], am[...])

    for d in range(5):
        use = mine[d] if d < 4 else jnp.logical_and(mine[d], n < 4)

        @pl.when(use)
        def _(d=d):
            take(rg.at[d], g_r.at[d])
            sg[d] = jnp.sum(rg[d], axis=0)
            row = pl.ds(pl.multiple_of(lows[d] * B + 8 * t, 8), 8)
            col = pl.ds(pl.multiple_of(highs[d] * B, B), B)
            local(sg.at[d], gw.at[row, col], y_r.at[lows[d]])
            for s in (1, 7, 2, 6, 3, 5, 4):
                send(sg.at[d], gw.at[row, col], y_s.at[d], y_r.at[lows[d]], k, lax.rem(n + s, COLS))

    for a in range(COLS):
        @pl.when(core == a % 2)
        def _(a=a):
            piece = gw.at[pl.ds(pl.multiple_of(a * B + 8 * t, 8), 8), a * B : K]
            take(piece, y_r.at[a])
            for s in range(1, CHIPS):
                send(piece, piece, a_s.at[a], a_r.at[a], 2 * lax.rem(t + s, CHIPS) + core, n)

    for s in range(1, ROWS):
        to = lax.rem(k + s, ROWS)
        rows = pl.ds(pl.multiple_of(32 * to, 32), 32)
        send(pd.at[rows], rd.at[k], d_s, d_r, to, n)
        send(pcx.at[rows], rc.at[k], c_s, c_r, to, n)
    own_rows = pl.ds(pl.multiple_of(32 * k, 32), 32)
    local(pd.at[own_rows], rd.at[k], d_r)
    local(pcx.at[own_rows], rc.at[k], c_r)

    def hand_over(a):
        @pl.when(core == a % 2)
        def _():
            take(gw.at[a * B : a * B + 120, a * B : K], a_r.at[a])
            panel = gw.at[a * B : (a + 1) * B, a * B : K]
            send(panel, panel, p_s.at[a], p_r.at[a], k + 1 - 2 * core, n)

    def arrived(a):
        @pl.when(core != a % 2)
        def _():
            take(gw.at[a * B : (a + 1) * B, a * B : K], p_r.at[a])

    def spread_products():
        take(rd, d_r)
        take(rc, c_r)
        sd[...] = jnp.sum(rd[...], axis=0)
        sc[...] = jnp.sum(rc[...], axis=0)
        for s in range(1, ROWS):
            send(sd, rhs.at[own_rows, B : 3 * B], e_s, e_r, lax.rem(k + s, ROWS), n)
        local(sd, rhs.at[own_rows, B : 3 * B], e_r)
        for h in range(2):
            for o in range(2):
                r_to = 4 * n + 2 * h + o
                piece = sc.at[:, h * B : (h + 1) * B]
                there = rhs.at[own_rows, 0:B]
                for s in range(1, COLS):
                    send(piece, there, f_s, f_r, r_to, lax.rem(n + s, COLS))

                @pl.when(r_to == k)
                def _():
                    local(piece, there, f_r)

                @pl.when(r_to != k)
                def _():
                    send(piece, there, f_s, f_r, r_to, n)

    hand_over(0)
    hand_over(1)

    @pl.loop(0, COLS)
    def _(p):
        for a in range(COLS):
            @pl.when(p == a)
            def _(a=a):
                if a + 2 < COLS:
                    hand_over(a + 2)
                if a == CD_STEP:
                    spread_products()
                arrived(a)
                r0, r1 = a * B, (a + 1) * B
                if a:
                    s = gw[r0:r1, r0:K] - dot_t(rr[0:r0, r0:r1], rr[0:r0, r0:K])
                    dd[...] = s[:, 0:B]
                    if a + 1 < COLS:
                        rr[r0:r1, r1:K] = s[:, B:]
                else:
                    dd[...] = gw[r0:r1, r0:r1]
                    rr[r0:r1, r1:K] = gw[r0:r1, r1:K]
        factor_block(dd, dr, lis.at[p])
        for a in range(COLS):
            @pl.when(p == a)
            def _(a=a):
                r0, r1 = a * B, (a + 1) * B
                rr[r0:r1, r0:r1] = dr[...]
                if a + 1 < COLS:
                    rr[r0:r1, r1:K] = dot(lis[a], rr[r0:r1, r1:K])

    mine_r = k // 4

    @pl.when(n >= mine_r)
    def _():
        tri[...] = rr[own_rows, pl.ds(pl.multiple_of(n * B, B), B)]

    @pl.when(n < mine_r)
    def _():
        tri[...] = jnp.zeros_like(tri)

    take(rhs.at[:, B : 3 * B], e_r)
    take(rhs.at[:, 0:B], f_r)
    for a in range(COLS):
        r0, r1 = a * B, (a + 1) * B
        s = rhs[r0:r1, :]
        x = dot(lis[a], s)
        rhs[r0:r1, :] = x
        if a + 1 < COLS:
            rhs[r1:K, :] -= dot_t(rr[r0:r1, r1:K], x)
    oo[...] = dot_t(rhs[:, 0:B], rhs[:, B : 3 * B])
    out[...] = oo[pl.ds(pl.multiple_of(64 * core, 64), 64), :]

    take(zb.at[0:7], z_s)
    for d in range(5):
        def left_share(d=d):
            @pl.when(mine[d])
            def _():
                take(rg.at[d, 0:15], g_s.at[d])
                take(rg.at[d, 0:7], y_s.at[d])

            @pl.when(jnp.logical_not(mine[d]))
            def _():
                take(rg.at[d, 0:16], g_s.at[d])

        if d < 4:
            left_share()
        else:
            pl.when(n < 4)(left_share)
    for a in range(COLS):
        @pl.when(core == a % 2)
        def _(a=a):
            take(gw.at[a * B : a * B + 120, a * B : K], a_s.at[a])
            take(gw.at[a * B : (a + 1) * B, a * B : K], p_s.at[a])
    take(rd.at[0:31], d_s)
    take(rc.at[0:31], c_s)
    take(rd.at[0:31], e_s)

    @pl.when(k // 4 == n)
    def _():
        take(rhs.at[0 : K - 32, 0:B], f_s)

    @pl.when(k // 4 != n)
    def _():
        take(rhs.at[:, 0:B], f_s)


def local_step(am, bm, ap, bp):
    f32 = jnp.float32
    vmem = pltpu.VMEM
    dma = pltpu.SemaphoreType.DMA
    return pl.pallas_call(
        kernel,
        out_shape=(jax.ShapeDtypeStruct((32, B), f32), jax.ShapeDtypeStruct((64, 256), f32)),
        in_specs=[pl.BlockSpec(memory_space=vmem)] * 4,
        out_specs=[pl.BlockSpec(memory_space=vmem)] * 2,
        scratch_shapes=[
            vmem((COLS, B, B), f32),
            vmem((5, B, B), f32),
            vmem((5, ROWS, 8, B), f32),
            vmem((5, 8, B), f32),
            vmem((K, K), f32),
            vmem((K, 256), f32),
            vmem((K, 256), f32),
            vmem((ROWS, 32, 256), f32),
            vmem((ROWS, 32, 256), f32),
            vmem((32, 256), f32),
            vmem((32, 256), f32),
            vmem((K, 3 * B), f32),
            vmem((K, K), f32),
            vmem((COLS, B, B), f32),
            vmem((B, B), f32),
            vmem((B, B), f32),
            vmem((B, 256), f32),
            dma, dma((COLS,)),
            dma((5,)), dma((5,)),
            dma((5,)), dma((COLS,)),
            dma((COLS,)), dma((COLS,)),
            dma((COLS,)), dma((COLS,)),
            dma, dma, dma, dma, dma, dma, dma, dma,
        ],
        compiler_params=pltpu.CompilerParams(
            collective_id=0, has_side_effects=True, vmem_limit_bytes=60 * 2**20
        ),
    )(am, bm, ap, bp)


def solution(mesh):
    spec = P("row", "col")
    return jax.shard_map(
        local_step, mesh=mesh, in_specs=(spec,) * 4, out_specs=(spec, spec), check_vma=False
    )
```

time: 579 us -> 136 us (0.23); the launches traced: 572 us -> 136 us
  other arithmetic: 265 us -> 0 us
  Pallas kernels: 0 us -> 132 us
  blocking collectives: 109 us -> 0 us
  waiting for transfers between devices: 78.9 us -> 0 us
  matrix products: 41.5 us -> 0 us
  local copies, waits for them, and re-layouts: 38.7 us -> 2.8 us
  between operations: 19.9 us -> 0.64 us
  starting transfers between devices: 18.2 us -> 0 us
    another operation x33 -> x0, other arithmetic: 258 us -> none  [the longest x30 172 us: local(): lower_factor = jnp.linalg.cholesky(gram_matrix)]
    pallas_call x0 -> x1, Pallas kernels: none -> 132 us  [local_step(): pl.pallas_call(kernel, out_shape=(jax.ShapeDtypeStruct((32, B), f32), jax...]
    all_to_all x3 -> x0, blocking collectives: 66.3 us -> none  [the longest x2 51.2 us: summed_on_arrival(): lax.all_to_all(blocks, axis, split_axis=0, concat_axis=0, tiled=True)]
    all_gather x1 -> x0, waiting for transfers between devices: 54.4 us -> none  [local(): gram_matrix = lax.all_gather(gram_rows, 'col', axis=0, tiled=True)]
    all_gather x2 -> x0, blocking collectives: 43.1 us -> none  [the longest x1 22.9 us: in_one_piece(): whole = lax.all_gather(both, axis, axis=dim, tiled=True)]
    another operation x29 -> x0, matrix products: 35.8 us -> none  [the longest x14 22.7 us: local(): lower_factor = jnp.linalg.cholesky(gram_matrix)]
    another operation x35 -> x0, local copies, waits for them, and re-layouts: 26.6 us -> none
    all_to_all x2 -> x0, waiting for transfers between devices: 24.4 us -> none  [the longest x1 24.4 us: summed_on_arrival(): lax.all_to_all(blocks, axis, split_axis=0, concat_axis=0, tiled=True)]
  transfers between devices with their start and end apart: 3 -> 0, of which waited for: 2 -> 0; matrix products, arithmetic and copies ran while one was open for 0% -> 0% of each run, Pallas kernels for 0% -> 0%
where the time goes in v1:
time: 136 us
  Pallas kernels  132 us (97%)
  local copies, waits for them, and re-layouts  2.8 us (2%)
    pallas_call x1, Pallas kernels, local_step(): pl.pallas_call(kernel, out_shape=(jax.ShapeDtypeStruct((32, B), f32), jax...  132 us
    unnamed x2, local copies, waits for them, and re-layouts  2.8 us

profile of v1, /device:TPU:3, one launch (start us, length us, event | category | flops | bytes accessed | tf_op | source)
XLA Modules:
  0.0 135.7 jit_solution(13156016885238491161)
XLA Ops:
  0.6 132.3 %shard_map.59 = (f32[32,128]{1,0:T(8,128)}, f32[64,256]{1,0:T(8,128)}) custom-call(f32[64,256]{1,0:T(8,128)} %am.1, f32[64,256]{1,0:T(8,128)} %bm.1, f32[64,128]{1,0:T(8,128)} %ap.1, f32[64,128]{1,0:T(8,128)} %bp.1), custom_call_target="tpu_custom_call" | custom-call | tf_op jit(solution)/shard_map/pallas_call | solution.py:305
  132.9 1.3 copy.8
  134.2 1.5 %copy.9 = f32[64,256]{1,0:T(8,128)} copy(f32[64,256]{1,0:T(8,128)} %get-tuple-element.5) | data formatting | bytes 131072

commit v2 on v1

v2 whole, which is shorter than its diff:
```python
import jax
import jax.numpy as jnp
from jax import lax
from jax.experimental import pallas as pl
from jax.experimental.pallas import tpu as pltpu
from jax.sharding import PartitionSpec as P

HIGHEST = lax.Precision.HIGHEST
MESH = pl.DeviceIdType.MESH
B = 128
ROWS = 32
COLS = 8
CHIPS = 16
K = COLS * B
PAIR_C_STEP = 1
PAIR_D_STEP = 3
SUM_C_STEP = 4
SUM_D_STEP = 5
SPREAD_STEP = 5
HAND_D_STEP = 7


def dot_t(a, b):
    return lax.dot_general(
        a, b, (((0,), (0,)), ((), ())), precision=HIGHEST, preferred_element_type=jnp.float32
    )


def dot(a, b):
    return jnp.dot(a, b, precision=HIGHEST, preferred_element_type=jnp.float32)


def split(x):
    high = x.astype(jnp.bfloat16)
    return high, (x - high.astype(jnp.float32)).astype(jnp.bfloat16)


def dot_split(a, b, dims):
    (ah, al), (bh, bl) = split(a), split(b)

    def part(x, y):
        return lax.dot_general(x, y, (dims, ((), ())), preferred_element_type=jnp.float32)

    return part(ah, bh) + (part(ah, bl) + part(al, bh))


def fast_t(a, b):
    return dot_split(a, b, ((0,), (0,)))


def fast(a, b):
    return dot_split(a, b, ((1,), (0,)))


def lane(x, k):
    return jnp.broadcast_to(x[:, k : k + 1], x.shape)


def sub(x, k):
    return jnp.broadcast_to(x[k : k + 1, :], x.shape)


def total(terms):
    while len(terms) > 1:
        odd = terms[len(terms) - len(terms) % 2 :]
        terms = [terms[m] + terms[m + 1] for m in range(0, len(terms) - 1, 2)] + odd
    return terms[0]


def factor_block(d_ref, r_ref, li_ref):
    srow = lax.broadcasted_iota(jnp.int32, (8, B), 0)
    lcol = lax.broadcasted_iota(jnp.int32, (8, B), 1)
    groups = B // 8
    left = [d_ref[8 * g : 8 * g + 8, :] for g in range(groups)]
    right = [jnp.where(lcol == srow + 8 * g, 1.0, 0.0).astype(jnp.float32) for g in range(groups)]
    cols = [lane(left[0], m) for m in range(8)]
    for i in range(groups):
        p, q = left[i], right[i]
        more = i + 1 < groups
        ahead = []
        if more:
            by = [lane(left[i + 1], 8 * i + m) for m in range(8)]
            later = [lane(left[i + 1], 8 * i + 8 + m) for m in range(8)]
            ahead = [lane(p, 8 * i + 8 + m) for m in range(8)]
        rp = jnp.zeros((8, B), jnp.float32)
        rq = rp
        for m in range(8):
            pivot = sub(cols[m], m)
            inv = 1.0 / pivot
            root = lax.rsqrt(pivot)
            f = jnp.where(srow == m, 1.0 - inv, cols[m] * inv)
            for c in range(m + 1, 8):
                cols[c] = cols[c] - f * sub(cols[c], m)
            pm, qm = sub(p, m), sub(q, m)
            rp = jnp.where(srow == m, pm * root, rp)
            rq = jnp.where(srow == m, qm * root, rq)
            p = p - f * pm
            q = q - f * qm
            ahead = [x - f * sub(x, m) for x in ahead]
        r_ref[8 * i : 8 * i + 8, :] = jnp.where(lcol >= srow + 8 * i, rp, 0.0)
        li_ref[8 * i : 8 * i + 8, :] = rq
        yp = [sub(p, m) for m in range(8)]
        yq = [sub(q, m) for m in range(8)]
        if more:
            cols = [later[c] - total([by[m] * sub(ahead[c], m) for m in range(8)]) for c in range(8)]
        for g in range(i + 1, groups):
            w = by if g == i + 1 else [lane(left[g], 8 * i + m) for m in range(8)]
            left[g] = left[g] - total([w[m] * yp[m] for m in range(8)])
            right[g] = right[g] - total([w[m] * yq[m] for m in range(8)])


def place(b):
    return b // 2 + 4 * (b % 2)


def held(a, parity):
    first = a + 1 if (a + 1) % 2 == parity else a + 2
    return (first // 2 + 4 * parity) * B, (4 + 4 * parity) * B


def kernel(
    am, bm, ap, bp, tri, out,
    av, bv, tv, ov, zb, pg, rg, sg, gc, gd, gw, pd, pcx, qd, qc, rd, rc, sd, sc, cz, dl, rhs, rr, lis, dd, dr, oo,
    z_s, z_r, w_s, g_s, g_r, y_s, y_r, yd_r, b_s, b_r, a_s, a_r, p_s, p_r,
    q_s, q_r, d_s, d_r, c_s, c_r, e_s, e_r, h_s, h_r, f_s, f_r, i_s, i_r, o_r, m_r,
):
    k = lax.axis_index("row")
    n = lax.axis_index("col")
    t = k // 2
    core = lax.rem(k, 2)

    pltpu.make_async_copy(am, av, m_r.at[0]).start()
    pltpu.make_async_copy(bm, bv, m_r.at[1]).start()
    barrier = pltpu.get_barrier_semaphore()
    for s in range(1, COLS):
        pl.semaphore_signal(barrier, inc=1, device_id=(k, lax.rem(n + s, COLS)), device_id_type=MESH)
    for s in range(1, ROWS):
        pl.semaphore_signal(barrier, inc=1, device_id=(lax.rem(k + s, ROWS), n), device_id_type=MESH)
    pl.semaphore_wait(barrier, COLS - 1 + ROWS - 1)

    def send(src, dst, ssem, rsem, row, col):
        pltpu.make_async_remote_copy(
            src_ref=src, dst_ref=dst, send_sem=ssem, recv_sem=rsem, device_id=(row, col), device_id_type=MESH
        ).start()

    def local(src, dst, sem):
        pltpu.make_async_copy(src, dst, sem).start()

    def take(ref, sem):
        pltpu.make_async_copy(ref, ref, sem).wait()

    def near(s):
        return lax.rem(n + s + COLS, COLS)

    def send_panels(steps, sem):
        for s in steps:
            send(bp, zb.at[n, 0:64], sem, z_r.at[n], k, near(s))
            send(ap, zb.at[n, 64:128], sem, z_r.at[n], k, near(s))

    send_panels((1, -1, 2, -2), z_s)
    local(bp, zb.at[n, 0:64], z_r.at[n])
    local(ap, zb.at[n, 64:128], z_r.at[n])
    lows, highs, mine = [], [], []
    for d in range(5):
        i, j = near(-(d // 2)), near((d + 1) // 2)
        lo, hi = jnp.minimum(i, j), jnp.maximum(i, j)
        lows.append(lo)
        highs.append(hi)
        mine.append(lax.rem(hi, 2) == core)

    def where_needed(d, body):
        if d < 4:
            body()
        else:
            pl.when(n < 4)(body)

    def share(d):
        def body():
            pg[d] = dot_t(zb[lows[d]], zb[highs[d]])
            to_core = lax.rem(highs[d], 2)
            for s in range(1, CHIPS):
                to = lax.rem(t + s, CHIPS)
                send(pg.at[d, pl.ds(pl.multiple_of(8 * to, 8), 8)], rg.at[d, k], g_s.at[d], g_r.at[d], 2 * to + to_core, n)
            own = pg.at[d, pl.ds(pl.multiple_of(8 * t, 8), 8)]

            @pl.when(mine[d])
            def _():
                local(own, rg.at[d, k], g_r.at[d])

            @pl.when(jnp.logical_not(mine[d]))
            def _():
                send(own, rg.at[d, k], g_s.at[d], g_r.at[d], 2 * t + 1 - core, n)

        where_needed(d, body)

    def add_up(d):
        def body():
            @pl.when(mine[d])
            def _():
                take(rg.at[d], g_r.at[d])
                sg[d] = jnp.sum(rg[d], axis=0)
                if d == 0:
                    there, sem = gc.at[n], yd_r.at[n]
                else:
                    row = pl.ds(pl.multiple_of(lows[d] * B + 8 * t, 8), 8)
                    pos = highs[d] // 2 + 4 * core
                    there, sem = gw.at[row, pl.ds(pl.multiple_of(pos * B, B), B)], y_r.at[lows[d]]
                local(sg.at[d], there, sem)
                for s in (1, -1, 2, -2, 3, -3, 4):
                    send(sg.at[d], there, y_s.at[d], sem, k, near(s))

        where_needed(d, body)

    rows8 = pl.ds(pl.multiple_of(8 * t, 8), 8)

    def send_diagonal(a):
        @pl.when(core == a % 2)
        def _():
            take(gc.at[a], yd_r.at[a])
            for s in range(1, ROWS):
                send(gc.at[a], gd.at[a, rows8], b_s.at[a], b_r.at[a], lax.rem(k + s, ROWS), n)
            local(gc.at[a], gd.at[a, rows8], b_r.at[a])

    def send_rows(a):
        for parity in range(2):
            c0, c1 = held(a, parity)
            if c0 < c1:
                @pl.when(core == parity)
                def _(c0=c0, c1=c1):
                    piece = gw.at[pl.ds(pl.multiple_of(a * B + 8 * t, 8), 8), c0:c1]
                    take(piece, y_r.at[a])
                    for s in range(1, CHIPS):
                        sem = a_r.at[a] if a else o_r.at[s]
                        to = 2 * lax.rem(t + s, CHIPS)
                        send(piece, piece, a_s.at[a], sem, to + core, n)
                        if a == 1:
                            send(piece, piece, p_s.at[a], p_r.at[a], to + 1 - core, n)
                    if a < 2:
                        send(piece, piece, p_s.at[a], p_r.at[a], k + 1 - 2 * core, n)

    take(zb.at[n], z_r.at[n])
    share(0)
    take(zb.at[near(1)], z_r.at[near(1)])
    share(1)
    add_up(0)
    take(zb.at[near(-1)], z_r.at[near(-1)])
    share(2)
    take(zb.at[near(2)], z_r.at[near(2)])
    share(3)
    take(zb.at[near(-2)], z_r.at[near(-2)])
    share(4)
    send_panels((3, -3, 4), w_s)
    send_diagonal(0)
    for d in range(1, 5):
        add_up(d)

    def form_products():
        take(av, m_r.at[0])
        take(bv, m_r.at[1])
        for s in (3, -3, 4):
            take(zb.at[near(s)], z_r.at[near(s)])
        for c in range(COLS):
            d_part = fast_t(zb[c, 64:128, :], bv[...])
            c_part = fast_t(zb[c, 0:64, :], av[...])
            for e in range(4):
                r = 4 * c + e
                pd[r % 2, r // 2] = d_part[32 * e : 32 * e + 32, :]
                pcx[r % 2, r // 2] = c_part[32 * e : 32 * e + 32, :]
        send(pcx.at[1 - core], qc, q_s.at[1], q_r.at[1], k + 1 - 2 * core, n)
        send(pd.at[1 - core], qd, q_s.at[0], q_r.at[0], k + 1 - 2 * core, n)

    own_rows = pl.ds(pl.multiple_of(32 * k, 32), 32)

    def hand_over(a):
        for parity in range(2):
            c0, c1 = held(a, parity)
            if c0 < c1:
                @pl.when(core == parity)
                def _(c0=c0, c1=c1):
                    if a == 0:
                        for s in range(1, CHIPS):
                            source = lax.rem(t - s + CHIPS, CHIPS)
                            piece = gw.at[pl.ds(pl.multiple_of(8 * source, 8), 8), c0:c1]
                            take(piece, o_r.at[s])
                            send(piece, piece, p_s.at[a], p_r.at[a], k + 1 - 2 * core, n)
                    else:
                        take(gw.at[a * B : a * B + 120, c0:c1], a_r.at[a])
                    if a > 1:
                        panel = gw.at[a * B : (a + 1) * B, c0:c1]
                        send(panel, panel, p_s.at[a], p_r.at[a], k + 1 - 2 * core, n)

    def arrived(a):
        for parity in range(2):
            c0, c1 = held(a, parity)
            if c0 < c1:
                @pl.when(core != parity)
                def _(c0=c0, c1=c1):
                    take(gw.at[a * B : (a + 1) * B, c0:c1], p_r.at[a])

    def pair_up(index, got, ours, there, ssem, rsem):
        take(got, q_r.at[index])
        got[...] += ours[core]
        for s in range(1, CHIPS):
            to = lax.rem(t + s, CHIPS)
            send(got.at[to], there.at[t], ssem, rsem, 2 * to + core, n)
        local(got.at[t], there.at[t], rsem)

    def sum_c():
        take(rc, c_r)
        sc[...] = jnp.sum(rc[...], axis=0)
        for s in (1, -1, 2, -2, 3, -3, 4):
            send(sc, cz.at[n], h_s, h_r, k, near(s))
        local(sc, cz.at[n], h_r)

    def sum_d():
        take(rd, d_r)
        sd[...] = jnp.sum(rd[...], axis=0)
        for s in range(1, CHIPS):
            send(sd, dl.at[core, t], e_s, e_r, 2 * lax.rem(t + s, CHIPS) + core, n)
        local(sd, dl.at[core, t], e_r)

    def hand_d():
        take(dl.at[core], e_r)
        send(dl.at[core], dl.at[core], i_s, i_r, k + 1 - 2 * core, n)

    def spread_products():
        take(cz, h_r)
        for s in range(ROWS):
            to = lax.rem(k + s, ROWS)
            half = pl.ds(pl.multiple_of(lax.rem(to // 2, 2) * B, B), B)
            piece, there = cz.at[to // 4, :, half], rhs.at[own_rows, 0:B]
            if s:
                send(piece, there, f_s, f_r, to, n)
            else:
                local(piece, there, f_r)

    @pl.loop(0, COLS)
    def _(p):
        for a in range(COLS):
            @pl.when(p == a)
            def _(a=a):
                if a == PAIR_C_STEP:
                    pair_up(1, qc, pcx, rc, c_s, c_r)
                if a == PAIR_D_STEP:
                    pair_up(0, qd, pd, rd, d_s, d_r)
                if a == SUM_C_STEP:
                    sum_c()
                if a == SUM_D_STEP:
                    sum_d()
                if a == HAND_D_STEP:
                    hand_d()
                take(gd.at[a], b_r.at[a])
                r0, r1 = a * B, (a + 1) * B
                if a:
                    u = rr[0:r0, r0:r1]
                    dd[...] = gd[a] - dot_t(u, u)
                else:
                    dd[...] = gd[0]
        factor_block(dd, dr, lis.at[p])
        for a in range(COLS):
            @pl.when(p == a)
            def _(a=a):
                r0, r1 = a * B, (a + 1) * B
                if a == SPREAD_STEP:
                    spread_products()
                rr[r0:r1, r0:r1] = dr[...]
                if a + 1 < COLS:
                    if a == 0:
                        send_rows(0)
                        form_products()
                        send_diagonal(1)
                        send_rows(1)
                        hand_over(0)
                    if a == 1:
                        hand_over(1)
                    arrived(a)
                    g = jnp.concatenate([gw[r0:r1, place(b) * B : (place(b) + 1) * B] for b in range(a + 1, COLS)], axis=1)
                    if a:
                        g = g - dot_t(rr[0:r0, r0:r1], rr[0:r0, r1:K])
                    rr[r0:r1, r1:K] = dot(lis[a], g)
                for after in {0: (2,), 1: range(3, COLS)}.get(a, ()):
                    send_diagonal(after)
                    if after + 1 < COLS:
                        send_rows(after)
                if 1 < a + 1 < COLS - 1:
                    hand_over(a + 1)

    mine_r = k // 4

    @pl.when(n >= mine_r)
    def _():
        tv[...] = rr[own_rows, pl.ds(pl.multiple_of(n * B, B), B)]

    @pl.when(n < mine_r)
    def _():
        tv[...] = jnp.zeros_like(tv)

    local(tv, tri, m_r.at[2])

    take(dl.at[1 - core], i_r)
    for r in range(ROWS):
        rhs[32 * r : 32 * r + 32, B : 3 * B] = dl[r % 2, r // 2]
    take(rhs.at[:, 0:B], f_r)
    for a in range(COLS):
        r0, r1 = a * B, (a + 1) * B
        s = rhs[r0:r1, :]
        x = fast(lis[a], s)
        rhs[r0:r1, :] = x
        if a + 1 < COLS:
            rhs[r1:K, :] -= fast_t(rr[r0:r1, r1:K], x)
    oo[...] = fast_t(rhs[:, 0:B], rhs[:, B : 3 * B])
    result = oo.at[pl.ds(pl.multiple_of(64 * core, 64), 64)]
    local(result, out, m_r.at[3])

    take(tv, m_r.at[2])
    take(ov, m_r.at[3])
    take(zb.at[0:4], z_s)
    take(zb.at[0:3], w_s)
    for d in range(5):
        def left_share(d=d):
            @pl.when(mine[d])
            def _():
                take(rg.at[d, 0:15], g_s.at[d])
                take(rg.at[d, 0:7], y_s.at[d])

            @pl.when(jnp.logical_not(mine[d]))
            def _():
                take(rg.at[d, 0:16], g_s.at[d])

        if d < 4:
            left_share()
        else:
            pl.when(n < 4)(left_share)
    for a in range(COLS):
        @pl.when(core == a % 2)
        def _(a=a):
            take(rg.at[0, 0:31], b_s.at[a])

        for parity in range(2):
            c0, c1 = held(a, parity)
            if c0 < c1:
                @pl.when(core == parity)
                def _(a=a, c0=c0, c1=c1):
                    take(gw.at[a * B : a * B + 120, c0:c1], a_s.at[a])
                    take(gw.at[a * B : (a + 1) * B, c0:c1], p_s.at[a])
    take(qd, q_s.at[0])
    take(qc, q_s.at[1])
    take(rd.at[0:15], d_s)
    take(rc.at[0:15], c_s)
    take(rd.at[0:15], e_s)
    take(rd, i_s)
    take(cz.at[0:7], h_s)
    take(rhs.at[0 : K - 32, 0:B], f_s)


def local_step(am, bm, ap, bp):
    f32 = jnp.float32
    vmem = pltpu.VMEM
    dma = pltpu.SemaphoreType.DMA
    return pl.pallas_call(
        kernel,
        out_shape=(jax.ShapeDtypeStruct((32, B), f32), jax.ShapeDtypeStruct((64, 256), f32)),
        in_specs=[pl.BlockSpec(memory_space=pl.ANY)] * 4,
        out_specs=[pl.BlockSpec(memory_space=pl.ANY)] * 2,
        scratch_shapes=[
            vmem((64, 256), f32),
            vmem((64, 256), f32),
            vmem((32, B), f32),
            vmem((64, 256), f32),
            vmem((COLS, B, B), f32),
            vmem((5, B, B), f32),
            vmem((5, ROWS, 8, B), f32),
            vmem((5, 8, B), f32),
            vmem((COLS, 8, B), f32),
            vmem((COLS, B, B), f32),
            vmem((K, K), f32),
            vmem((2, CHIPS, 32, 256), f32),
            vmem((2, CHIPS, 32, 256), f32),
            vmem((CHIPS, 32, 256), f32),
            vmem((CHIPS, 32, 256), f32),
            vmem((CHIPS, 32, 256), f32),
            vmem((CHIPS, 32, 256), f32),
            vmem((32, 256), f32),
            vmem((32, 256), f32),
            vmem((COLS, 32, 256), f32),
            vmem((2, CHIPS, 32, 256), f32),
            vmem((K, 3 * B), f32),
            vmem((K, K), f32),
            vmem((COLS, B, B), f32),
            vmem((B, B), f32),
            vmem((B, B), f32),
            vmem((B, 256), f32),
            dma, dma((COLS,)), dma,
            dma((5,)), dma((5,)),
            dma((5,)), dma((COLS,)), dma((COLS,)),
            dma((COLS,)), dma((COLS,)),
            dma((COLS,)), dma((COLS,)),
            dma((COLS,)), dma((COLS,)),
            dma((2,)), dma((2,)),
            dma, dma, dma, dma, dma, dma, dma, dma, dma, dma, dma, dma,
            dma((CHIPS,)), dma((4,)),
        ],
        compiler_params=pltpu.CompilerParams(
            collective_id=0, has_side_effects=True, vmem_limit_bytes=60 * 2**20
        ),
    )(am, bm, ap, bp)


def solution(mesh):
    spec = P("row", "col")
    return jax.shard_map(
        local_step, mesh=mesh, in_specs=(spec,) * 4, out_specs=(spec, spec), check_vma=False
    )
```

time: 136 us -> 87.4 us (0.64)
  Pallas kernels: 132 us -> 83.6 us
    pallas_call x1, Pallas kernels: 132 us -> 83.6 us  [local_step(): pl.pallas_call(kernel, out_shape=(jax.ShapeDtypeStruct((32, B), f32), jax...]
where the time goes in v2:
time: 87.4 us; the launch traced here: 87 us
  Pallas kernels  83.6 us (96%)
  local copies, waits for them, and re-layouts  2.8 us (3%)
    pallas_call x1, Pallas kernels, local_step(): pl.pallas_call(kernel, out_shape=(jax.ShapeDtypeStruct((32, B), f32), jax...  83.6 us
    unnamed x2, local copies, waits for them, and re-layouts  2.8 us

profile of v2, /device:TPU:3, one launch (start us, length us, event | category | flops | bytes accessed | tf_op | source)
XLA Modules:
  0.0 87.0 jit_solution(205859054156380624)
XLA Ops:
  0.6 83.6 %shard_map.59 = (f32[32,128]{1,0:T(8,128)}, f32[64,256]{1,0:T(8,128)}) custom-call(f32[64,256]{1,0:T(8,128)} %am.1, f32[64,256]{1,0:T(8,128)} %bm.1, f32[64,128]{1,0:T(8,128)} %ap.1, f32[64,128]{1,0:T(8,128)} %bp.1), custom_call_target="tpu_custom_call" | custom-call | tf_op jit(solution)/shard_map/pallas_call | solution.py:460
  84.2 1.3 %copy.8 = f32[32,128]{1,0:T(8,128)} copy(f32[32,128]{1,0:T(8,128)} %get-tuple-element.4) | data formatting | bytes 32768
  85.5 1.5 %copy.9 = f32[64,256]{1,0:T(8,128)} copy(f32[64,256]{1,0:T(8,128)} %get-tuple-element.5) | data formatting | bytes 131072

commit v3 on v2

--- a/solution.py
+++ b/solution.py
@@ -12,12 +12,11 @@
 COLS = 8
 CHIPS = 16
 K = COLS * B
-PAIR_C_STEP = 1
-PAIR_D_STEP = 3
+PAIR_C_STEP = 2
+PAIR_D_STEP = 4
 SUM_C_STEP = 4
-SUM_D_STEP = 5
-SPREAD_STEP = 5
-HAND_D_STEP = 7
+SUM_D_STEP = 6
+SPREAD_STEP = 6
 
 
 def dot_t(a, b):
@@ -120,7 +119,7 @@
 
 def kernel(
     am, bm, ap, bp, tri, out,
-    av, bv, tv, ov, zb, pg, rg, sg, gc, gd, gw, pd, pcx, qd, qc, rd, rc, sd, sc, cz, dl, rhs, rr, lis, dd, dr, oo,
+    av, bv, tv, zb, pg, rg, sg, gc, gd, gw, pd, pcx, qd, qc, rd, rc, sd, sc, cz, rhs, rr, lis, dd, dr, oo,
     z_s, z_r, w_s, g_s, g_r, y_s, y_r, yd_r, b_s, b_r, a_s, a_r, p_s, p_r,
     q_s, q_r, d_s, d_r, c_s, c_r, e_s, e_r, h_s, h_r, f_s, f_r, i_s, i_r, o_r, m_r,
 ):
@@ -233,9 +232,9 @@
                         sem = a_r.at[a] if a else o_r.at[s]
                         to = 2 * lax.rem(t + s, CHIPS)
                         send(piece, piece, a_s.at[a], sem, to + core, n)
-                        if a == 1:
+                        if a in (1, 2):
                             send(piece, piece, p_s.at[a], p_r.at[a], to + 1 - core, n)
-                    if a < 2:
+                    if a < 3:
                         send(piece, piece, p_s.at[a], p_r.at[a], k + 1 - 2 * core, n)
 
     take(zb.at[n], z_r.at[n])
@@ -285,7 +284,7 @@
                             send(piece, piece, p_s.at[a], p_r.at[a], k + 1 - 2 * core, n)
                     else:
                         take(gw.at[a * B : a * B + 120, c0:c1], a_r.at[a])
-                    if a > 1:
+                    if a > 2:
                         panel = gw.at[a * B : (a + 1) * B, c0:c1]
                         send(panel, panel, p_s.at[a], p_r.at[a], k + 1 - 2 * core, n)
 
@@ -315,13 +314,11 @@
     def sum_d():
         take(rd, d_r)
         sd[...] = jnp.sum(rd[...], axis=0)
-        for s in range(1, CHIPS):
-            send(sd, dl.at[core, t], e_s, e_r, 2 * lax.rem(t + s, CHIPS) + core, n)
-        local(sd, dl.at[core, t], e_r)
-
-    def hand_d():
-        take(dl.at[core], e_r)
-        send(dl.at[core], dl.at[core], i_s, i_r, k + 1 - 2 * core, n)
+        there = rhs.at[own_rows, B : 2 * B]
+        for s in range(1, ROWS):
+            to = lax.rem(k + s, ROWS)
+            send(sd.at[:, pl.ds(pl.multiple_of(lax.rem(to, 2) * B, B), B)], there, e_s, e_r, to, n)
+        local(sd.at[:, pl.ds(pl.multiple_of(core * B, B), B)], there, e_r)
 
     def spread_products():
         take(cz, h_r)
@@ -334,6 +331,11 @@
             else:
                 local(piece, there, f_r)
 
+    def blocks(a):
+        row = slice(a * B, (a + 1) * B)
+        rest = [gw[row, place(b) * B : (place(b) + 1) * B] for b in range(a + 1, COLS)]
+        return jnp.concatenate([gd[a]] + rest, axis=1)
+
     @pl.loop(0, COLS)
     def _(p):
         for a in range(COLS):
@@ -343,12 +345,8 @@
                     pair_up(1, qc, pcx, rc, c_s, c_r)
                 if a == PAIR_D_STEP:
                     pair_up(0, qd, pd, rd, d_s, d_r)
-                if a == SUM_C_STEP:
-                    sum_c()
                 if a == SUM_D_STEP:
                     sum_d()
-                if a == HAND_D_STEP:
-                    hand_d()
                 take(gd.at[a], b_r.at[a])
                 r0, r1 = a * B, (a + 1) * B
                 if a:
@@ -361,6 +359,8 @@
             @pl.when(p == a)
             def _(a=a):
                 r0, r1 = a * B, (a + 1) * B
+                if a == SUM_C_STEP:
+                    sum_c()
                 if a == SPREAD_STEP:
                     spread_products()
                 rr[r0:r1, r0:r1] = dr[...]
@@ -371,19 +371,20 @@
                         send_diagonal(1)
                         send_rows(1)
                         hand_over(0)
-                    if a == 1:
-                        hand_over(1)
+                    if a in (1, 2):
+                        hand_over(a)
                     arrived(a)
-                    g = jnp.concatenate([gw[r0:r1, place(b) * B : (place(b) + 1) * B] for b in range(a + 1, COLS)], axis=1)
                     if a:
-                        g = g - dot_t(rr[0:r0, r0:r1], rr[0:r0, r1:K])
+                        g = blocks(a)[:, B:] - dot_t(rr[0:r0, r0:r1], rr[0:r0, r1:K])
+                    else:
+                        g = blocks(a)[:, B:]
                     rr[r0:r1, r1:K] = dot(lis[a], g)
                 for after in {0: (2,), 1: range(3, COLS)}.get(a, ()):
                     send_diagonal(after)
                     if after + 1 < COLS:
                         send_rows(after)
-                if 1 < a + 1 < COLS - 1:
-                    hand_over(a + 1)
+                for after in {2: (3,), 3: (4,), 4: (5,), 5: (6,)}.get(a, ()):
+                    hand_over(after)
 
     mine_r = k // 4
 
@@ -397,23 +398,29 @@
 
     local(tv, tri, m_r.at[2])
 
-    take(dl.at[1 - core], i_r)
-    for r in range(ROWS):
-        rhs[32 * r : 32 * r + 32, B : 3 * B] = dl[r % 2, r // 2]
-    take(rhs.at[:, 0:B], f_r)
+    take(rhs.at[:, B : 2 * B], e_r)
     for a in range(COLS):
         r0, r1 = a * B, (a + 1) * B
-        s = rhs[r0:r1, :]
-        x = fast(lis[a], s)
-        rhs[r0:r1, :] = x
+        x = fast(lis[a], rhs[r0:r1, B : 2 * B])
+        rhs[r0:r1, B : 2 * B] = x
         if a + 1 < COLS:
-            rhs[r1:K, :] -= fast_t(rr[r0:r1, r1:K], x)
-    oo[...] = fast_t(rhs[:, 0:B], rhs[:, B : 3 * B])
-    result = oo.at[pl.ds(pl.multiple_of(64 * core, 64), 64)]
-    local(result, out, m_r.at[3])
+            rhs[r1:K, B : 2 * B] -= fast_t(rr[r0:r1, r1:K], x)
+    for a in reversed(range(COLS)):
+        r0, r1 = a * B, (a + 1) * B
+        x = rhs[r0:r1, B : 2 * B]
+        if a + 1 < COLS:
+            x = x - fast(rr[r0:r1, r1:K], rhs[r1:K, B : 2 * B])
+        rhs[r0:r1, B : 2 * B] = fast_t(lis[a], x)
+    take(rhs.at[:, 0:B], f_r)
+    oo[...] = fast_t(rhs[:, 0:B], rhs[:, B : 2 * B])
+    half = out.at[:, pl.ds(pl.multiple_of(core * B, B), B)]
+    send(oo.at[pl.ds(pl.multiple_of(64 * (1 - core), 64), 64)], half, i_s, i_r, k + 1 - 2 * core, n)
+    local(oo.at[pl.ds(pl.multiple_of(64 * core, 64), 64)], half, m_r.at[3])
 
     take(tv, m_r.at[2])
-    take(ov, m_r.at[3])
+    take(oo.at[0:64], m_r.at[3])
+    take(oo.at[0:64], i_r)
+    take(oo.at[0:64], i_s)
     take(zb.at[0:4], z_s)
     take(zb.at[0:3], w_s)
     for d in range(5):
@@ -447,17 +454,21 @@
     take(qc, q_s.at[1])
     take(rd.at[0:15], d_s)
     take(rc.at[0:15], c_s)
-    take(rd.at[0:15], e_s)
-    take(rd, i_s)
+    take(rhs.at[0 : K - 32, B : 2 * B], e_s)
     take(cz.at[0:7], h_s)
     take(rhs.at[0 : K - 32, 0:B], f_s)
+
+
+def hand_on(tri, cross, tri_out, cross_out):
+    tri_out[...] = tri[...]
+    cross_out[...] = cross[...]
 
 
 def local_step(am, bm, ap, bp):
     f32 = jnp.float32
     vmem = pltpu.VMEM
     dma = pltpu.SemaphoreType.DMA
-    return pl.pallas_call(
+    results = pl.pallas_call(
         kernel,
         out_shape=(jax.ShapeDtypeStruct((32, B), f32), jax.ShapeDtypeStruct((64, 256), f32)),
         in_specs=[pl.BlockSpec(memory_space=pl.ANY)] * 4,
@@ -466,7 +477,6 @@
             vmem((64, 256), f32),
             vmem((64, 256), f32),
             vmem((32, B), f32),
-            vmem((64, 256), f32),
             vmem((COLS, B, B), f32),
             vmem((5, B, B), f32),
             vmem((5, ROWS, 8, B), f32),
@@ -483,13 +493,12 @@
             vmem((32, 256), f32),
             vmem((32, 256), f32),
             vmem((COLS, 32, 256), f32),
-            vmem((2, CHIPS, 32, 256), f32),
-            vmem((K, 3 * B), f32),
+            vmem((K, 2 * B), f32),
             vmem((K, K), f32),
             vmem((COLS, B, B), f32),
             vmem((B, B), f32),
             vmem((B, B), f32),
-            vmem((B, 256), f32),
+            vmem((B, B), f32),
             dma, dma((COLS,)), dma,
             dma((5,)), dma((5,)),
             dma((5,)), dma((COLS,)), dma((COLS,)),
@@ -504,6 +513,12 @@
             collective_id=0, has_side_effects=True, vmem_limit_bytes=60 * 2**20
         ),
     )(am, bm, ap, bp)
+    return pl.pallas_call(
+        hand_on,
+        out_shape=(jax.ShapeDtypeStruct((32, B), f32), jax.ShapeDtypeStruct((64, 256), f32)),
+        in_specs=[pl.BlockSpec(memory_space=vmem)] * 2,
+        out_specs=[pl.BlockSpec(memory_space=vmem)] * 2,
+    )(*results)
 
 
 def solution(mesh):

time: 87.4 us -> 87.6 us (level)
  local copies, waits for them, and re-layouts: 2.8 us -> 0 us
  Pallas kernels: 83.6 us -> 85.8 us
    unnamed x2 -> x0, local copies, waits for them, and re-layouts: 2.8 us -> none
    pallas_call x0 -> x1, Pallas kernels: none -> 1.5 us  [local_step(): pl.pallas_call(hand_on, out_shape=(jax.ShapeDtypeStruct((32, B), f32), ja...]
where the time goes in v3:
time: 87.6 us; the launch traced here: 86.4 us
  Pallas kernels  85.8 us (98%)
    pallas_call x1, Pallas kernels, local_step(): pl.pallas_call(kernel, out_shape=(jax.ShapeDtypeStruct((32, B), f32), jax...  84.3 us

profile of v3, /device:TPU:3, one launch (start us, length us, event | category | flops | bytes accessed | tf_op | source)
XLA Modules:
  0.0 86.4 jit_solution(4004937325842616785)
XLA Ops:
  0.6 84.3 %shard_map.59 = (f32[32,128]{1,0:T(8,128)}, f32[64,256]{1,0:T(8,128)}) custom-call(f32[64,256]{1,0:T(8,128)} %am.1, f32[64,256]{1,0:T(8,128)} %bm.1, f32[64,128]{1,0:T(8,128)} %ap.1, f32[64,128]{1,0:T(8,128)} %bp.1), custom_call_target="tpu_custom_call" | custom-call | tf_op jit(solution)/shard_map/pallas_call | solution.py:471
  85.0 1.5 %shard_map.60 = (f32[32,128]{1,0:T(8,128)}, f32[64,256]{1,0:T(8,128)}) custom-call(f32[32,128]{1,0:T(8,128)} %get-tuple-element.4.tri, f32[64,256]{1,0:T(8,128)} %get-tuple-element.5.cross), custom_call_target="tpu_custom_call" | custom-call | tf_op jit(solution)/shard_map/pallas_call | solution.py:516

commit v4 on v3

--- a/solution.py
+++ b/solution.py
@@ -12,11 +12,11 @@
 COLS = 8
 CHIPS = 16
 K = COLS * B
-PAIR_C_STEP = 2
-PAIR_D_STEP = 4
+PAIR_C_STEP = 1
+PAIR_D_STEP = 3
 SUM_C_STEP = 4
-SUM_D_STEP = 6
-SPREAD_STEP = 6
+SUM_D_STEP = 5
+SPREAD_STEP = 5
 
 
 def dot_t(a, b):
@@ -232,9 +232,9 @@
                         sem = a_r.at[a] if a else o_r.at[s]
                         to = 2 * lax.rem(t + s, CHIPS)
                         send(piece, piece, a_s.at[a], sem, to + core, n)
-                        if a in (1, 2):
+                        if a == 1:
                             send(piece, piece, p_s.at[a], p_r.at[a], to + 1 - core, n)
-                    if a < 3:
+                    if a < 2:
                         send(piece, piece, p_s.at[a], p_r.at[a], k + 1 - 2 * core, n)
 
     take(zb.at[n], z_r.at[n])
@@ -284,7 +284,7 @@
                             send(piece, piece, p_s.at[a], p_r.at[a], k + 1 - 2 * core, n)
                     else:
                         take(gw.at[a * B : a * B + 120, c0:c1], a_r.at[a])
-                    if a > 2:
+                    if a > 1:
                         panel = gw.at[a * B : (a + 1) * B, c0:c1]
                         send(panel, panel, p_s.at[a], p_r.at[a], k + 1 - 2 * core, n)
 
@@ -345,6 +345,8 @@
                     pair_up(1, qc, pcx, rc, c_s, c_r)
                 if a == PAIR_D_STEP:
                     pair_up(0, qd, pd, rd, d_s, d_r)
+                if a == SUM_C_STEP:
+                    sum_c()
                 if a == SUM_D_STEP:
                     sum_d()
                 take(gd.at[a], b_r.at[a])
@@ -359,8 +361,6 @@
             @pl.when(p == a)
             def _(a=a):
                 r0, r1 = a * B, (a + 1) * B
-                if a == SUM_C_STEP:
-                    sum_c()
                 if a == SPREAD_STEP:
                     spread_products()
                 rr[r0:r1, r0:r1] = dr[...]
@@ -371,7 +371,7 @@
                         send_diagonal(1)
                         send_rows(1)
                         hand_over(0)
-                    if a in (1, 2):
+                    if a == 1:
                         hand_over(a)
                     arrived(a)
                     if a:
@@ -383,7 +383,7 @@
                     send_diagonal(after)
                     if after + 1 < COLS:
                         send_rows(after)
-                for after in {2: (3,), 3: (4,), 4: (5,), 5: (6,)}.get(a, ()):
+                for after in {1: (2,), 2: (3,), 3: (4,), 4: (5,), 5: (6,)}.get(a, ()):
                     hand_over(after)
 
     mine_r = k // 4
@@ -399,19 +399,13 @@
     local(tv, tri, m_r.at[2])
 
     take(rhs.at[:, B : 2 * B], e_r)
+    take(rhs.at[:, 0:B], f_r)
     for a in range(COLS):
         r0, r1 = a * B, (a + 1) * B
-        x = fast(lis[a], rhs[r0:r1, B : 2 * B])
-        rhs[r0:r1, B : 2 * B] = x
+        x = fast(lis[a], rhs[r0:r1, :])
+        rhs[r0:r1, :] = x
         if a + 1 < COLS:
-            rhs[r1:K, B : 2 * B] -= fast_t(rr[r0:r1, r1:K], x)
-    for a in reversed(range(COLS)):
-        r0, r1 = a * B, (a + 1) * B
-        x = rhs[r0:r1, B : 2 * B]
-        if a + 1 < COLS:
-            x = x - fast(rr[r0:r1, r1:K], rhs[r1:K, B : 2 * B])
-        rhs[r0:r1, B : 2 * B] = fast_t(lis[a], x)
-    take(rhs.at[:, 0:B], f_r)
+            rhs[r1:K, :] -= fast_t(rr[r0:r1, r1:K], x)
     oo[...] = fast_t(rhs[:, 0:B], rhs[:, B : 2 * B])
     half = out.at[:, pl.ds(pl.multiple_of(core * B, B), B)]
     send(oo.at[pl.ds(pl.multiple_of(64 * (1 - core), 64), 64)], half, i_s, i_r, k + 1 - 2 * core, n)

time: 87.6 us -> 85.9 us (0.981)
  no operation moved by 1% of the time
where the time goes in v4:
time: 85.9 us; the launch traced here: 85.6 us
  Pallas kernels  85 us (99%)
    pallas_call x1, Pallas kernels, local_step(): pl.pallas_call(kernel, out_shape=(jax.ShapeDtypeStruct((32, B), f32), jax...  83.5 us

profile of v4, /device:TPU:3, one launch (start us, length us, event | category | flops | bytes accessed | tf_op | source)
XLA Modules:
  0.0 85.6 jit_solution(9905217028395564164)
XLA Ops:
  0.6 83.5 %shard_map.59 = (f32[32,128]{1,0:T(8,128)}, f32[64,256]{1,0:T(8,128)}) custom-call(f32[64,256]{1,0:T(8,128)} %am.1, f32[64,256]{1,0:T(8,128)} %bm.1, f32[64,128]{1,0:T(8,128)} %ap.1, f32[64,128]{1,0:T(8,128)} %bp.1), custom_call_target="tpu_custom_call" | custom-call | tf_op jit(solution)/shard_map/pallas_call | solution.py:465
  84.1 1.5 %shard_map.60 = (f32[32,128]{1,0:T(8,128)}, f32[64,256]{1,0:T(8,128)}) custom-call(f32[32,128]{1,0:T(8,128)} %get-tuple-element.4.tri, f32[64,256]{1,0:T(8,128)} %get-tuple-element.5.cross), custom_call_target="tpu_custom_call" | custom-call | tf_op jit(solution)/shard_map/pallas_call | solution.py:510
